TPU v7x, 128 devices: a whole 4x4x4 slice. The times are simulated.
128 devices in a mesh: dp: 16 (over z, x), expert: 8 (over y, core).
Axes of the slice: x: 4, y: 4, z: 4, core: 2. Of those that a mesh axis runs over, the one named last changes fastest.
Arguments:
- grads: bfloat16 [16, 4096, 6144], P('dp', None, 'expert'), parts along dimension 2, may hold values from -16 to 16
- error: bfloat16 [16, 4096, 6144], P('dp', None, 'expert'), parts along dimension 2, may hold values from -6 to 6
- q_start: float32 [6144, 32], P('expert'), parts along dimension 0, may hold values from -6 to 6
- bucket: float32 [16, 524288], P('dp', 'expert'), parts along dimension 1, may hold values from -6 to 6
Outputs:
- update: float32 [4096, 6144], P(None, 'expert'), parts along dimension 1
- new_error: bfloat16 [16, 4096, 6144], P('dp', None, 'expert'), parts along dimension 2
- bucket_mean: float32 [524288], P(('expert', 'dp')), parts along dimension 0
There are 8 independent parts, one for each index of `expert`. A program takes and returns all parts, laid end to end along the dimension named above; each array names one. Nothing has to cross between parts.
All inputs are finite; a program needn't handle non-finite values.
Results may differ from a plain program's by a relative error of at most 0.02.
Values may be sent and summed in bfloat16 or wider, within the bound.
A program may use at most 128 MiB of HBM per device.

v0:
```python
import jax
import jax.numpy as jnp
from jax import lax
from jax.sharding import PartitionSpec as P

ITERS = 2


def on_device(grads, error, q_start, bucket):
    replicas = lax.axis_size("dp")
    compensated = (grads[0].astype(jnp.float32) + error[0].astype(jnp.float32)).astype(jnp.bfloat16)
    bucket_share = (
        lax.psum_scatter(
            bucket[0].astype(jnp.bfloat16), "dp", scatter_dimension=0, tiled=True
        ).astype(jnp.float32)
        / replicas
    )
    factor_q = q_start
    p_half = None
    for step in range(ITERS):
        q_half = factor_q.astype(jnp.bfloat16)
        local_p = jnp.dot(compensated, q_half, preferred_element_type=jnp.float32)
        factor_p = lax.psum(local_p, "dp") / replicas
        gram = jnp.dot(factor_p.T, factor_p, precision=lax.Precision.HIGHEST)
        lower = jnp.linalg.cholesky(gram)
        p_half = jax.scipy.linalg.solve_triangular(lower, factor_p.T, lower=True).T.astype(
            jnp.bfloat16
        )
        local_q = lax.dot_general(
            compensated, p_half, (((0,), (0,)), ((), ())), preferred_element_type=jnp.float32
        )
        factor_q = lax.psum(local_q.astype(jnp.bfloat16), "dp").astype(jnp.float32) / replicas
        if step + 1 < ITERS:
            factor_q = factor_q / jnp.sqrt(
                jnp.sum(factor_q * factor_q, axis=0, keepdims=True) + 1e-06
            )
    update = jnp.dot(p_half.astype(jnp.float32), factor_q.T, precision=lax.Precision.HIGHEST)
    new_error = (compensated.astype(jnp.float32) - update).astype(jnp.bfloat16)[None]
    return (update, new_error, bucket_share)


def solution(mesh):
    return jax.shard_map(
        on_device,
        mesh=mesh,
        in_specs=(
            P("dp", None, "expert"),
            P("dp", None, "expert"),
            P("expert", None),
            P("dp", "expert"),
        ),
        out_specs=(P(None, "expert"), P("dp", None, "expert"), P(("expert", "dp"))),
        check_vma=False,
    )
```

profile of v0, /device:TPU:0, one launch (start us, length us, event | category | flops | bytes accessed | tf_op | source)
XLA Modules:
  0.0 393.4 jit_solution(18393514925062783348)
XLA Ops:
  7.2 0.0 copy-start.2
  7.2 0.0 all-reduce.5.cloned.1.call-start
  7.2 6.2 %fusion = bf16[4096,768]{1,0:T(8,128)(2,1)S(1)} fusion(bf16[1,4096,768]{2,1,0:T(8,128)(2,1)} %param.8, bf16[1,4096,768]{2,1,0:T(8,128)(2,1)} %param.7), kind=kLoop, calls=%fused_computation.2 | loop fusion | flops 12582912 | bytes 18874368 | tf_op jit(solution)/shard_map/convert_element_type | solution.py:11
  13.4 0.0 copy-start
  13.4 2.7 copy-done
  16.1 0.0 copy-done.2
  16.1 0.0 copy-start.1
  16.1 2.7 fusion.21
  18.9 0.0 all-reduce.5.cloned.1.call-update
  18.9 0.0 all-reduce.9.cloned.1.call-start
  18.9 0.0 copy-done.1
  19.0 1.3 convert_reduce_fusion
  20.3 0.0 all-reduce.9.cloned.1.call-update
  20.3 0.0 all-reduce.7.cloned.1.call-start
  20.4 87.0 %all-reduce.5.cloned.1.call-done = f32[4096,32]{0,1:T(8,128)} async-done(((f32[4096,32]{0,1:T(8,128)}), f32[4096,32]{0,1:T(8,128)}) %all-reduce.5.cloned.1.call-update) | async-done | bytes 524304 | tf_op jit(solution)/shard_map/psum | solution.py:23
  107.3 1.8 fusion.8
  109.1 0.1 copy.9
  109.2 2.9 cholesky.44
  112.2 0.6 compare_reduce_fusion.1
  112.8 0.7 fusion.23
  113.5 2.4 custom-call.6
  115.9 1.7 convolution_convert_fusion.1
  117.6 0.0 copy-start.3
  117.6 3.9 convolution_convert_fusion.3
  121.5 72.2 %psum.29 = bf16[768,32]{0,1:T(8,128)(2,1)S(1)} all-reduce(bf16[768,32]{0,1:T(8,128)(2,1)S(1)} %convolution_convert_fusion.3), channel_id=1, replica_groups=mesh['dp'=16,'expert'=8] {'dp'}, use_global_device_ids=true, to_apply=%region_3.0 | all-reduce | flops 24576 | bytes 98304 | tf_op jit(solution)/shard_map/psum | solution.py:32
  193.7 0.1 multiply_reduce_fusion
  193.8 5.5 %fusion.17 = f32[4096,32]{0,1:T(8,128)} fusion(bf16[4096,768]{1,0:T(8,128)(2,1)} %copy-done, bf16[768,32]{0,1:T(8,128)(2,1)S(1)} %psum.29, f32[32]{0:T(128)S(1)} %add_sqrt_fusion), kind=kOutput, calls=%fused_computation.27 | convolution fusion | flops 201424896 | bytes 6865024 | tf_op jit(solution)/shard_map/dot_general | solution.py:22
  199.4 0.0 all-reduce.7.cloned.1.call-update
  199.4 0.0 copy-done.3
  199.4 0.6 dynamic-slice
  200.6 0.0 all-reduce.9.cloned.1.call-done
  200.7 1.3 convert_multiply_fusion.1
  202.0 80.0 %all-reduce.7.cloned.1.call-done = f32[4096,32]{0,1:T(8,128)} async-done(((f32[4096,32]{0,1:T(8,128)}), f32[4096,32]{0,1:T(8,128)}) %all-reduce.7.cloned.1.call-update) | async-done | bytes 524304 | tf_op jit(solution)/shard_map/psum | solution.py:23
  282.0 1.8 fusion.5
  283.8 0.1 copy.10
  283.9 2.9 cholesky.55
  286.8 0.6 compare_reduce_fusion
  287.4 0.7 fusion.24
  288.1 2.4 custom-call.7
  290.5 1.7 convolution_convert_fusion
  292.2 3.9 convolution_convert_fusion.2
  296.1 72.2 %psum.31 = bf16[768,32]{0,1:T(8,128)(2,1)S(1)} all-reduce(bf16[768,32]{0,1:T(8,128)(2,1)S(1)} %convolution_convert_fusion.2), channel_id=1, replica_groups=mesh['dp'=16,'expert'=8] {'dp'}, use_global_device_ids=true, to_apply=%region_6.9 | all-reduce | flops 24576 | bytes 98304 | tf_op jit(solution)/shard_map/psum | solution.py:32
  368.3 8.0 %fusion.14 = f32[4096,768]{1,0:T(8,128)} fusion(bf16[32,4096]{1,0:T(8,128)(2,1)S(1)} %convolution_convert_fusion, bf16[768,32]{0,1:T(8,128)(2,1)S(1)} %psum.31), kind=kOutput, calls=%fused_computation.21 | convolution fusion | flops 1208008704 | bytes 12894208 | tf_op jit(solution)/shard_map/dot_general | solution.py:37
  376.4 10.5 %fusion.1 = bf16[1,4096,768]{2,1,0:T(8,128)(2,1)} fusion(f32[4096,768]{1,0:T(8,128)} %fusion.14, bf16[4096,768]{1,0:T(8,128)(2,1)} %copy-done), kind=kLoop, calls=%fused_computation.3 | loop fusion | flops 9437184 | bytes 25165824 | tf_op jit(solution)/shard_map/broadcast_in_dim | solution.py:38
  (5 shorter events, 0.1 us)
Async XLA Ops:
  7.2 9.0 %copy-start.2 = (f32[768,32]{0,1:T(8,128)S(1)}, f32[768,32]{0,1:T(8,128)}, u32[]{:S(2)}) copy-start(f32[768,32]{0,1:T(8,128)} %param.9) | copy-start | bytes 294916
  7.2 100.2 %all-reduce.5.cloned.1.call-start = ((), (), s32[]{:S(2)}) async-start(), calls=%async_computation | async-start | bytes 1048576 | tf_op jit(solution)/shard_map/psum | solution.py:23
  13.4 2.7 copy-start
  16.1 2.8 copy-start.1
  18.9 181.8 %all-reduce.9.cloned.1.call-start = ((), (), s32[]{:S(2)}) async-start(), calls=%async_computation.2 | async-start | bytes 262144
  20.3 261.7 %all-reduce.7.cloned.1.call-start = ((), (), s32[]{:S(2)}) async-start(), calls=%async_computation.1 | async-start | bytes 1048576 | tf_op jit(solution)/shard_map/psum | solution.py:23
  117.6 81.8 %copy-start.3 = (u32[128]{0:T(128)S(1)}, u32[128]{0:T(128)}, u32[]{:S(2)}) copy-start(u32[128]{0:T(128)} %constant.49) | copy-start | bytes 1540
Sparse Core Ops, SparseCore 0:
  19.0 88.2 all-reduce.4
  110.5 82.5 all-reduce.8
  199.5 82.4 all-reduce.6
where the time goes:
time: 394 us; the launch traced here: 393 us
  waiting for transfers between devices  167 us (42%)
  blocking collectives  144 us (37%)
  other arithmetic  32.8 us (8%)
  matrix products  31 us (8%)
  between operations  14.5 us (4%)
    psum x2, waiting for transfers between devices, on_device(): factor_p = lax.psum(local_p, 'dp') / replicas  167 us
    psum x2, blocking collectives, on_device(): lax.psum(local_q.astype(jnp.bfloat16), 'dp').astype(jnp.float32) / replicas  144 us
    broadcast_in_dim x1, other arithmetic, on_device(): (compensated.astype(jnp.float32) - update).astype(jnp.bfloat16)[None]  10.5 us
    dot_general x2, matrix products, on_device(): local_p = jnp.dot(compensated, q_half, preferred_element_type=jnp.float32)  8.25 us
    dot_general x1, matrix products, on_device(): jnp.dot(p_half.astype(jnp.float32), factor_q.T, precision=lax.Precision.H...  8.02 us
  transfers between devices with their start and end apart: 3, of which 2 were waited for; matrix products, arithmetic and copies ran while one was open for 6% of the time, Pallas kernels for 0%

commit v1 on v0

v1 whole, which is shorter than its diff:
```python
import functools

import jax
import jax.numpy as jnp
from jax import lax
from jax.experimental import pallas as pl
from jax.experimental.pallas import tpu as pltpu
from jax.sharding import PartitionSpec as P

ITERS = 2
MESH = pl.DeviceIdType.MESH
F32 = jnp.float32
BF16 = jnp.bfloat16


def offsets(side):
    near = lambda d: min(d, side - d)
    every = [(dz, dx) for dz in range(side) for dx in range(side) if (dz, dx) != (0, 0)]
    return sorted(every, key=lambda o: (-(near(o[0]) + near(o[1])), o))


def split3(x):
    hi = x.astype(BF16)
    rest = x - hi.astype(F32)
    mid = rest.astype(BF16)
    low = (rest - mid.astype(F32)).astype(BF16)
    return hi, mid, low


def inverse_cholesky(gram):
    n = gram.shape[0]
    lanes = 128
    row_id = lax.broadcasted_iota(jnp.int32, (n, lanes), 0)
    lane_id = lax.broadcasted_iota(jnp.int32, (n, lanes), 1)
    eye = (lane_id == row_id + n).astype(F32)
    work = jnp.concatenate([gram, jnp.zeros((n, lanes - n), F32)], axis=1) + eye
    out = jnp.zeros((n, lanes), F32)
    for k in range(n):
        row = work[k : k + 1, :]
        pivot = jnp.broadcast_to(row[:, k : k + 1], (1, lanes))
        out = jnp.where(row_id == k, row / jnp.sqrt(pivot), out)
        if k + 1 < n:
            column = jnp.broadcast_to(work[:, k : k + 1], (n, lanes))
            column = jnp.where(row_id > k, column, 0.0)
            work = work - column * (row / pivot)
    return out[:, n : 2 * n]


def iterate_kernel(
    n,
    side,
    grads,
    error,
    q_start,
    bucket,
    comp,
    p_out,
    q_out,
    mean_out,
    g_buf,
    e_buf,
    p_send,
    p_recv,
    p_all,
    q_x,
    b_buf,
    b_recv,
    load_sem,
    b_send_sem,
    b_recv_sem,
    rs_send_sem,
    rs_recv_sem,
    ag_send_sem,
    ag_recv_sem,
    q_send_sem,
    q_recv_sem,
):
    me = lax.axis_index("dp")
    my_z, my_x = lax.div(me, side), lax.rem(me, side)
    order = offsets(side)
    peers = [lax.rem(my_z + dz, side) * side + lax.rem(my_x + dx, side) for dz, dx in order]
    rows = comp.shape[1]
    rank = q_start.shape[0]
    inv_n = 1.0 / n

    def remote(src, dst, send, recv, peer):
        return pltpu.make_async_remote_copy(
            src_ref=src, dst_ref=dst, send_sem=send, recv_sem=recv, device_id={"dp": peer}, device_id_type=MESH
        )

    barrier = pltpu.get_barrier_semaphore()
    for peer in peers:
        pl.semaphore_signal(barrier, inc=1, device_id={"dp": peer}, device_id_type=MESH)

    def loads(j):
        part = pl.ds(pl.multiple_of(j * rows, rows), rows)
        return (
            pltpu.make_async_copy(grads.at[part], g_buf.at[j], load_sem.at[0, j]),
            pltpu.make_async_copy(error.at[part], e_buf.at[j], load_sem.at[1, j]),
        )

    for j in peers + [me]:
        for copy in loads(j):
            copy.start()

    b_buf[...] = bucket[...].astype(BF16)
    pl.semaphore_wait(barrier, n - 1)

    for peer in peers:
        remote(b_buf.at[peer], b_recv.at[me], b_send_sem.at[peer], b_recv_sem.at[me], peer).start()

    q_half = q_start[...].astype(BF16)
    for it in range(ITERS):
        def block(j):
            if it == 0:
                for copy in loads(j):
                    copy.wait()
                comp[j] = (g_buf[j].astype(F32) + e_buf[j].astype(F32)).astype(BF16)
            return lax.dot_general(q_half, comp[j], (((1,), (1,)), ((), ())), preferred_element_type=F32)

        for peer in peers:
            p_send[it, peer] = block(peer).astype(BF16)
            remote(
                p_send.at[it, peer],
                p_recv.at[it, me],
                rs_send_sem.at[it, peer],
                rs_recv_sem.at[it, me],
                peer,
            ).start()
        total = block(me)
        for peer in reversed(peers):
            remote(
                p_send.at[it, peer], p_recv.at[it, peer], rs_send_sem.at[it, peer], rs_recv_sem.at[it, peer], peer
            ).wait_recv()
            total = total + p_recv[it, peer].astype(F32)

        def mine(j):
            return p_all.at[it, :, pl.ds(pl.multiple_of(j * rows, rows), rows)]

        p_all[it, :, pl.ds(pl.multiple_of(me * rows, rows), rows)] = (total * inv_n).astype(BF16)
        for peer in peers:
            remote(mine(me), mine(me), ag_send_sem.at[it, peer], ag_recv_sem.at[it, me], peer).start()
        for peer in reversed(peers):
            remote(mine(me), mine(peer), ag_send_sem.at[it, peer], ag_recv_sem.at[it, peer], peer).wait_recv()

        factor_p = p_all[it]
        gram = lax.dot_general(factor_p, factor_p, (((1,), (1,)), ((), ())), preferred_element_type=F32)
        hi, mid, low = split3(inverse_cholesky(gram))
        p_hat = (
            jnp.dot(hi, factor_p, preferred_element_type=F32)
            + jnp.dot(mid, factor_p, preferred_element_type=F32)
            + jnp.dot(low, factor_p, preferred_element_type=F32)
        ).astype(BF16)

        local_q = jnp.zeros((rank, comp.shape[2]), F32)
        for j in range(n):
            local_q = local_q + jnp.dot(
                p_hat[:, j * rows : (j + 1) * rows], comp[j], preferred_element_type=F32
            )
        half = comp.shape[2] // 2
        parts = [local_q[:, :half], local_q[:, half:]]
        for stage in range(2):
            started = []
            for h in range(2):
                along_x = (h + stage) % 2 == 0
                mine_at = my_x if along_x else my_z
                q_x[it, stage, h, mine_at] = parts[h].astype(BF16)
                for d in (2, 1, 3):
                    at = lax.rem(mine_at + d, side)
                    peer = my_z * side + at if along_x else at * side + my_x
                    send = q_send_sem.at[it, stage, h, d]
                    slot = q_x.at[it, stage, h, mine_at]
                    remote(slot, slot, send, q_recv_sem.at[it, stage, h, mine_at], peer).start()
                    started.append((slot, q_x.at[it, stage, h, at], send, q_recv_sem.at[it, stage, h, at], peer))
            for args in started:
                remote(*args).wait_recv()
            for h in range(2):
                parts[h] = sum(q_x[it, stage, h, s].astype(F32) for s in range(side))
            for args in started:
                remote(*args).wait_send()
        factor_q = jnp.concatenate(parts, axis=1) * inv_n

        for peer in peers:
            remote(
                p_send.at[it, peer], p_recv.at[it, peer], rs_send_sem.at[it, peer], rs_recv_sem.at[it, peer], peer
            ).wait_send()
            remote(mine(me), mine(peer), ag_send_sem.at[it, peer], ag_recv_sem.at[it, peer], peer).wait_send()
        if it + 1 < ITERS:
            factor_q = factor_q / jnp.sqrt(jnp.sum(factor_q * factor_q, axis=1, keepdims=True) + 1e-06)
            q_half = factor_q.astype(BF16)
        else:
            p_out[...] = p_hat
            q_out[...] = factor_q

    share = b_buf[me].astype(F32)
    for peer in peers:
        copy = remote(b_buf.at[peer], b_recv.at[peer], b_send_sem.at[peer], b_recv_sem.at[peer], peer)
        copy.wait_recv()
        share = share + b_recv[peer].astype(F32)
        copy.wait_send()
    mean_out[...] = share * inv_n


def output_kernel(comp, p_hat, factor_q, update, new_error, u_buf, n_buf, sem):
    blocks, rows, _ = comp.shape
    hi, mid, low = split3(factor_q[...])
    right = jnp.concatenate([hi, mid, low], axis=0)

    def stores(j):
        slot = j % 2
        part = pl.ds(j * rows, rows)
        return (
            pltpu.make_async_copy(u_buf.at[slot], update.at[part], sem.at[0, slot]),
            pltpu.make_async_copy(n_buf.at[slot], new_error.at[part], sem.at[1, slot]),
        )

    for j in range(blocks):
        slot = j % 2
        if j >= 2:
            for copy in stores(j - 2):
                copy.wait()
        left = p_hat[:, j * rows : (j + 1) * rows]
        left = jnp.concatenate([left, left, left], axis=0)
        value = lax.dot_general(left, right, (((0,), (0,)), ((), ())), preferred_element_type=F32)
        u_buf[slot] = value
        n_buf[slot] = (comp[j].astype(F32) - value).astype(BF16)
        for copy in stores(j):
            copy.start()
    for j in (blocks - 2, blocks - 1):
        for copy in stores(j):
            copy.wait()


def on_device(n, side, grads, error, q_start, bucket):
    depth, width = grads.shape[1:]
    rank = q_start.shape[1]
    rows = depth // n
    shares = bucket.shape[1] // n // 128
    vmem = pl.BlockSpec(memory_space=pltpu.VMEM)
    anywhere = pl.BlockSpec(memory_space=pltpu.HBM)
    sds = jax.ShapeDtypeStruct
    dma = pltpu.SemaphoreType.DMA
    comp, p_hat, factor_q, mean = pl.pallas_call(
        functools.partial(iterate_kernel, n, side),
        out_shape=(
            sds((n, rows, width), BF16),
            sds((rank, depth), BF16),
            sds((rank, width), F32),
            sds((shares, 128), F32),
        ),
        in_specs=[anywhere, anywhere, vmem, vmem],
        out_specs=(vmem, vmem, vmem, vmem),
        scratch_shapes=[
            pltpu.VMEM((n, rows, width), BF16),
            pltpu.VMEM((n, rows, width), BF16),
            pltpu.VMEM((ITERS, n, rank, rows), BF16),
            pltpu.VMEM((ITERS, n, rank, rows), BF16),
            pltpu.VMEM((ITERS, rank, depth), BF16),
            pltpu.VMEM((ITERS, 2, 2, side, rank, width // 2), BF16),
            pltpu.VMEM((n, shares, 128), BF16),
            pltpu.VMEM((n, shares, 128), BF16),
            dma((2, n)),
            dma((n,)),
            dma((n,)),
            dma((ITERS, n)),
            dma((ITERS, n)),
            dma((ITERS, n)),
            dma((ITERS, n)),
            dma((ITERS, 2, 2, side)),
            dma((ITERS, 2, 2, side)),
        ],
        compiler_params=pltpu.CompilerParams(
            collective_id=0, has_side_effects=True, vmem_limit_bytes=40 << 20
        ),
        name="iterate",
    )(grads[0], error[0], q_start.T, bucket.reshape(n, shares, 128))

    update, new_error = pl.pallas_call(
        output_kernel,
        out_shape=(sds((depth, width), F32), sds((depth, width), BF16)),
        in_specs=[vmem, vmem, vmem],
        out_specs=(anywhere, anywhere),
        scratch_shapes=[
            pltpu.VMEM((2, rows, width), F32),
            pltpu.VMEM((2, rows, width), BF16),
            dma((2, 2)),
        ],
        compiler_params=pltpu.CompilerParams(vmem_limit_bytes=16 << 20),
        name="outputs",
    )(comp, p_hat, factor_q)
    return update, new_error[None], mean.reshape(-1)


def solution(mesh):
    n = mesh.shape["dp"]
    side = next(s for s in range(1, n + 1) if s * s == n)
    return jax.shard_map(
        functools.partial(on_device, n, side),
        mesh=mesh,
        in_specs=(
            P("dp", None, "expert"),
            P("dp", None, "expert"),
            P("expert", None),
            P("dp", "expert"),
        ),
        out_specs=(P(None, "expert"), P("dp", None, "expert"), P(("expert", "dp"))),
        check_vma=False,
    )
```

time: 394 us -> 78.6 us (0.20)
  waiting for transfers between devices: 167 us -> 0 us
  blocking collectives: 144 us -> 0 us
  Pallas kernels: 0 us -> 72.5 us
  other arithmetic: 32.8 us -> 0 us
  matrix products: 31 us -> 0 us
  between operations: 14.5 us -> 0.66 us
    psum x2 -> x0, waiting for transfers between devices: 167 us -> none  [on_device(): factor_p = lax.psum(local_p, 'dp') / replicas]
    psum x2 -> x0, blocking collectives: 144 us -> none  [on_device(): lax.psum(local_q.astype(jnp.bfloat16), 'dp').astype(jnp.float32) / replicas]
    pallas_call x0 -> x2, Pallas kernels: none -> 72.5 us  [the longest x1 61.6 us: on_device(): pl.pallas_call(functools.partial(iterate_kernel, n, side), out_shape=(sds...]
    dot_general x7 -> x0, matrix products: 27.7 us -> none  [the longest x2 8.25 us: on_device(): local_p = jnp.dot(compensated, q_half, preferred_element_type=jnp.float32)]
    another operation x10 -> x0, other arithmetic: 13.4 us -> none  [the longest x6 7.19 us: on_device(): lower = jnp.linalg.cholesky(gram)]
    broadcast_in_dim x1 -> x0, other arithmetic: 10.5 us -> none  [on_device(): (compensated.astype(jnp.float32) - update).astype(jnp.bfloat16)[None]]
    convert_element_type x2 -> x0, other arithmetic: 7.53 us -> none  [the longest x1 6.2 us: on_device(): (grads[0].astype(jnp.float32) + error[0].astype(jnp.float32)).astype(jnp....]
  transfers between devices with their start and end apart: 3 -> 0, of which waited for: 2 -> 0; matrix products, arithmetic and copies ran while one was open for 6% -> 0% of each run, Pallas kernels for 0% -> 0%
where the time goes in v1:
time: 78.6 us; the launch traced here: 78.4 us
  Pallas kernels  72.5 us (92%)
  local copies, waits for them, and re-layouts  5.23 us (7%)
    pallas_call x1, Pallas kernels, on_device(): pl.pallas_call(functools.partial(iterate_kernel, n, side), out_shape=(sds...  61.6 us
    pallas_call x1, Pallas kernels, on_device(): pl.pallas_call(output_kernel, out_shape=(sds((depth, width), F32), sds((d...  10.9 us
    unnamed x7, local copies, waits for them, and re-layouts  5.23 us

profile of v1, /device:TPU:0, one launch (start us, length us, event | category | flops | bytes accessed | tf_op | source)
XLA Modules:
  0.0 78.4 jit_solution(5908037762659600954)
XLA Ops:
  0.6 0.0 copy-start
  0.6 2.8 %copy-done = bf16[1,4096,768]{2,1,0:T(8,128)(2,1)S(1)} copy-done((bf16[1,4096,768]{2,1,0:T(8,128)(2,1)S(1)}, bf16[1,4096,768]{2,1,0:T(8,128)(2,1)}, u32[]{:S(2)}) %copy-start) | copy-done | bytes 6291480
  3.4 0.0 copy-start.1
  3.4 0.9 %copy-done.1 = f32[1,65536]{1,0:T(1,128)S(1)} copy-done((f32[1,65536]{1,0:T(1,128)S(1)}, f32[1,65536]{1,0:T(1,128)}, u32[]{:S(2)}) %copy-start.1) | copy-done | bytes 262168
  4.4 0.0 copy-start.2
  4.4 0.9 %copy-done.2 = f32[768,32]{0,1:T(8,128)S(1)} copy-done((f32[768,32]{0,1:T(8,128)S(1)}, f32[768,32]{0,1:T(8,128)}, u32[]{:S(2)}) %copy-start.2) | copy-done | bytes 98328
  5.3 61.6 %iterate.1 = (bf16[16,256,768]{2,1,0:T(8,128)(2,1)S(1)}, bf16[32,4096]{1,0:T(8,128)(2,1)S(1)}, f32[32,768]{1,0:T(8,128)S(1)}, f32[32,128]{1,0:T(8,128)S(1)}) custom-call(bf16[4096,768]{1,0:T(8,128)(2,1)S(1)} %bitcast.6, bf16[4096,768]{1,0:T(8,128)(2,1)} %bitcast.10, f32[32,768]{1,0:T(8,128)S(1)} %bitcast.8, f32[16,32,128]{2,1,0:T(8,128)S(1)} %bitcast.7), custom_call_target="tpu_custom_call" | custom-call | tf_op jit(solution)/shard_map/iterate/pallas_call | solution.py:243
  66.9 10.9 %outputs.1 = (f32[4096,768]{1,0:T(8,128)}, bf16[4096,768]{1,0:T(8,128)(2,1)}) custom-call(bf16[16,256,768]{2,1,0:T(8,128)(2,1)S(1)} %get-tuple-element.9.comp, bf16[32,4096]{1,0:T(8,128)(2,1)S(1)} %get-tuple-element.10.p_hat, f32[32,768]{1,0:T(8,128)S(1)} %get-tuple-element.11.factor_q), custom_call_target="tpu_custom_call" | custom-call | tf_op jit(solution)/shard_map/outputs/pallas_call | solution.py:278
  77.8 0.6 copy.8
Async XLA Ops:
  0.6 2.8 %copy-start = (bf16[1,4096,768]{2,1,0:T(8,128)(2,1)S(1)}, bf16[1,4096,768]{2,1,0:T(8,128)(2,1)}, u32[]{:S(2)}) copy-start(bf16[1,4096,768]{2,1,0:T(8,128)(2,1)} %param.4) | copy-start | bytes 18874372
  3.4 0.9 %copy-start.1 = (f32[1,65536]{1,0:T(1,128)S(1)}, f32[1,65536]{1,0:T(1,128)}, u32[]{:S(2)}) copy-start(f32[1,65536]{1,0:T(1,128)} %param.7) | copy-start | bytes 786436
  4.4 0.9 %copy-start.2 = (f32[768,32]{0,1:T(8,128)S(1)}, f32[768,32]{0,1:T(8,128)}, u32[]{:S(2)}) copy-start(f32[768,32]{0,1:T(8,128)} %param.6) | copy-start | bytes 294916

commit v2 on v1

v2 whole, which is shorter than its diff:
```python
import contextlib
import functools

import jax
import jax.numpy as jnp
from jax import lax
from jax.experimental import pallas as pl
from jax.experimental.pallas import tpu as pltpu
from jax.sharding import PartitionSpec as P

ITERS = 2
MESH = pl.DeviceIdType.MESH
F32 = jnp.float32
BF16 = jnp.bfloat16
AHEAD = 6
TRACE = False


def scope(name):
    return jax.named_scope(name) if TRACE else contextlib.nullcontext()


def runs(items, sizes):
    out = []
    for size in sizes:
        out.append(items[:size])
        items = items[size:]
    assert not items
    return out


def offsets(side):
    near = lambda d: min(d, side - d)
    every = [(dz, dx) for dz in range(side) for dx in range(side) if (dz, dx) != (0, 0)]
    return sorted(every, key=lambda o: (-(near(o[0]) + near(o[1])), o))


def split3(x):
    hi = x.astype(BF16)
    rest = x - hi.astype(F32)
    mid = rest.astype(BF16)
    low = (rest - mid.astype(F32)).astype(BF16)
    return hi, mid, low


def inverse_cholesky(gram, block=8):
    n, lanes, tile = gram.shape[0], 128, 8
    row_id = lax.broadcasted_iota(jnp.int32, (n, lanes), 0)
    lane_id = lax.broadcasted_iota(jnp.int32, (n, lanes), 1)
    eye = (lane_id == row_id + n).astype(F32)
    work = jnp.concatenate([gram, jnp.zeros((n, lanes - n), F32)], axis=1) + eye
    work = [work[tile * i : tile * (i + 1)] for i in range(n // tile)]
    out = [jnp.zeros((tile, lanes), F32) for _ in work]
    tile_row = row_id[:tile]
    for s in range(0, n, block):
        rows = [work[k // tile][k % tile : k % tile + 1] for k in range(s, s + block)]
        pivots = [
            [jnp.broadcast_to(rows[i][:, s + j : s + j + 1], (1, lanes)) for j in range(i + 1)] for i in range(block)
        ]
        rest = range((s + block) // tile, n // tile)
        columns = {
            (t, i): jnp.broadcast_to(work[t][:, s + i : s + i + 1], (tile, lanes)) for t in rest for i in range(block)
        }
        factor, inverse = {}, []
        for p in range(block):
            inverse.append(1.0 / pivots[p][p])
            for i in range(p + 1, block):
                factor[i, p] = pivots[i][p] * inverse[p]
                for j in range(p + 1, i + 1):
                    pivots[i][j] = pivots[i][j] - factor[i, p] * pivots[j][p]
                rows[i] = rows[i] - factor[i, p] * rows[p]
        for p in range(block):
            t, at = divmod(s + p, tile)
            out[t] = jnp.where(tile_row == at, rows[p] / jnp.sqrt(pivots[p][p]), out[t])
        solved = [rows[p] * inverse[p] for p in range(block)]
        for p in reversed(range(block)):
            for i in range(p + 1, block):
                solved[p] = solved[p] - factor[i, p] * solved[i]
        for t in rest:
            for i in range(block):
                work[t] = work[t] - columns[t, i] * solved[i]
    return jnp.concatenate(out, axis=0)[:, n : 2 * n]


def iterate_kernel(
    n,
    side,
    grads,
    error,
    q_start,
    bucket,
    comp,
    p_out,
    q_out,
    mean_out,
    comp_t,
    g_buf,
    e_buf,
    p_send,
    p_recv,
    p_all,
    q_x,
    q0_buf,
    b0_buf,
    b_buf,
    b_recv,
    load_sem,
    small_sem,
    b_send_sem,
    b_recv_sem,
    rs_send_sem,
    rs_recv_sem,
    ag_send_sem,
    ag_recv_sem,
    q_send_sem,
    q_recv_sem,
):
    me = lax.axis_index("dp")
    my_z, my_x = lax.div(me, side), lax.rem(me, side)
    order = offsets(side)
    peers = [lax.rem(my_z + dz, side) * side + lax.rem(my_x + dx, side) for dz, dx in order]
    rows = comp.shape[1]
    rank = q_start.shape[0]
    inv_n = 1.0 / n

    def remote(src, dst, send, recv, peer):
        return pltpu.make_async_remote_copy(
            src_ref=src, dst_ref=dst, send_sem=send, recv_sem=recv, device_id={"dp": peer}, device_id_type=MESH
        )

    barrier = pltpu.get_barrier_semaphore()
    for peer in peers:
        pl.semaphore_signal(barrier, inc=1, device_id={"dp": peer}, device_id_type=MESH)

    def loads(j):
        part = pl.ds(pl.multiple_of(j * rows, rows), rows)
        return (
            pltpu.make_async_copy(grads.at[part], g_buf.at[j], load_sem.at[0, j]),
            pltpu.make_async_copy(error.at[part], e_buf.at[j], load_sem.at[1, j]),
        )

    every = peers + [me]
    small = (
        pltpu.make_async_copy(q_start, q0_buf, small_sem.at[0]),
        pltpu.make_async_copy(bucket, b0_buf, small_sem.at[1]),
    )
    with scope("issue"):
        for j in every[:AHEAD]:
            for copy in loads(j):
                copy.start()
            if j is every[0]:
                small[0].start()
    def rs_copy(it, peer, slot):
        return remote(
            p_send.at[it, peer], p_recv.at[it, slot], rs_send_sem.at[it, peer], rs_recv_sem.at[it, slot], peer
        )

    def ag_copy(it, peer, slot):
        return remote(p_all.at[it, me], p_all.at[it, slot], ag_send_sem.at[it, peer], ag_recv_sem.at[it, slot], peer)

    def bucket_copy(peer, slot):
        return remote(b_buf.at[peer], b_recv.at[slot], b_send_sem.at[peer], b_recv_sem.at[slot], peer)

    for it in range(ITERS):
        with scope(f"p_local{it}"):
            loaded = 0
            for at, run in enumerate(runs(every, (1, 2, 3, 3, 3, 3, 1) if it == 0 else (5, 6, 5))):
                if it == 0:
                    with scope("load"):
                        for j in run:
                            for copy in loads(j):
                                copy.wait()
                        loaded += len(run)
                        for j in every[AHEAD + loaded - len(run) : AHEAD + loaded]:
                            for copy in loads(j):
                                copy.start()
                    for j in run:
                        comp[j] = g_buf[j] + e_buf[j]
                        comp_t[j] = comp[j].T
                    if at == 0:
                        small[0].wait()
                        q_half = q0_buf[...].astype(BF16)
                blocks = [jnp.dot(q_half, comp_t[j], preferred_element_type=F32) for j in run]
                for j, part in zip(run, blocks):
                    if j is me:
                        total = part
                    else:
                        p_send[it, j] = part.astype(BF16)
                if it > 0 or at > 1:
                    for j in run:
                        if j is not me:
                            rs_copy(it, j, me).start()
                elif at == 1:
                    with scope("entry"):
                        pl.semaphore_wait(barrier, n - 1)
                    for j in every[:loaded]:
                        rs_copy(it, j, me).start()
                    small[1].start()
        if it == ITERS - 1:
            with scope("bucket"):
                for peer in peers:
                    bucket_copy(peer, peer).wait_recv()
                share = b_buf[me].astype(F32)
                for peer in peers:
                    share = share + b_recv[peer].astype(F32)
                mean_out[...] = share * inv_n
        with scope(f"rs{it}"):
            for run in runs(peers[::-1], (10, 5)):
                for peer in run:
                    rs_copy(it, peer, peer).wait_recv()
                for peer in run:
                    total = total + p_recv[it, peer].astype(F32)
            p_all[it, me] = (total * inv_n).astype(BF16)

        with scope(f"ag{it}"):
            for peer in peers:
                ag_copy(it, peer, me).start()
            gram = jnp.zeros((rank, rank), F32)
            raw_q = jnp.zeros((rank, comp.shape[2]), F32)
            for run in runs(every[::-1], (5, 6, 4, 1)):
                for j in run:
                    if j is not me:
                        ag_copy(it, j, j).wait_recv()
                for j in run:
                    part = p_all[it, j]
                    gram = gram + lax.dot_general(part, part, (((1,), (1,)), ((), ())), preferred_element_type=F32)
                    raw_q = raw_q + jnp.dot(part, comp[j], preferred_element_type=F32)
        if it == 0:
            with scope("bucket"):
                small[1].wait()
                b_buf[...] = b0_buf[...].astype(BF16)
                for peer in peers:
                    bucket_copy(peer, me).start()
        with scope(f"cholesky{it}"):
            inverse = inverse_cholesky(gram)

        half = comp.shape[2] // 2
        for stage in range(2):
            with scope(f"q_send{it}_{stage}"):
                started = []
                for h in range(2):
                    if stage == 0:
                        part = jnp.dot(
                            inverse,
                            raw_q[:, h * half : (h + 1) * half],
                            preferred_element_type=F32,
                            precision=lax.Precision.HIGHEST,
                        )
                    else:
                        part = parts[h]
                    along_x = (h + stage) % 2 == 0
                    mine_at = my_x if along_x else my_z
                    slot = q_x.at[it, stage, h, mine_at]
                    slot[...] = part.astype(BF16)
                    for d in (2, 1, 3):
                        at = lax.rem(mine_at + d, side)
                        peer = my_z * side + at if along_x else at * side + my_x
                        send = q_send_sem.at[it, stage, h, d]
                        remote(slot, slot, send, q_recv_sem.at[it, stage, h, mine_at], peer).start()
                        started.append((slot, q_x.at[it, stage, h, at], send, q_recv_sem.at[it, stage, h, at], peer))
            if stage == 0 and it == ITERS - 1:
                with scope("p_hat"):
                    pieces = split3(inverse)
                    for j in range(n):
                        p_out[:, j * rows : (j + 1) * rows] = sum(
                            jnp.dot(piece, p_all[it, j], preferred_element_type=F32) for piece in pieces
                        ).astype(BF16)
            with scope(f"q_wait{it}_{stage}"):
                for args in started:
                    remote(*args).wait_recv()
            parts = [sum(q_x[it, stage, h, s].astype(F32) for s in range(side)) for h in range(2)]
            for args in started:
                remote(*args).wait_send()
        factor_q = jnp.concatenate(parts, axis=1) * inv_n
        if it + 1 < ITERS:
            factor_q = factor_q / jnp.sqrt(jnp.sum(factor_q * factor_q, axis=1, keepdims=True) + 1e-06)
            q_half = factor_q.astype(BF16)
        else:
            q_out[...] = factor_q

    with scope("sends"):
        for peer in peers:
            for it in range(ITERS):
                rs_copy(it, peer, peer).wait_send()
                ag_copy(it, peer, peer).wait_send()
            bucket_copy(peer, peer).wait_send()


def output_kernel(comp, p_hat, factor_q, mean, update, new_error, mean_out, u_buf, n_buf, sem, mean_sem):
    blocks, rows, _ = comp.shape
    mean_copy = pltpu.make_async_copy(mean, mean_out, mean_sem)
    mean_copy.start()
    hi, mid, low = split3(factor_q[...])
    right = jnp.concatenate([hi, mid, low], axis=0)

    slots = u_buf.shape[0]

    def stores(j):
        slot = j % slots
        part = pl.ds(j * rows, rows)
        return (
            pltpu.make_async_copy(u_buf.at[slot], update.at[part], sem.at[0, slot]),
            pltpu.make_async_copy(n_buf.at[slot], new_error.at[part], sem.at[1, slot]),
        )

    for j in range(blocks):
        slot = j % slots
        if j >= slots:
            with scope("stores"):
                for copy in stores(j - slots):
                    copy.wait()
        with scope("block"):
            left = p_hat[:, j * rows : (j + 1) * rows]
            left = jnp.concatenate([left, left, left], axis=0)
            value = lax.dot_general(left, right, (((0,), (0,)), ((), ())), preferred_element_type=F32)
            u_buf[slot] = value
            n_buf[slot] = (comp[j].astype(F32) - value).astype(BF16)
        for copy in stores(j):
            copy.start()
    with scope("last"):
        for j in range(blocks - slots, blocks):
            for copy in stores(j):
                copy.wait()
    mean_copy.wait()


def in_hbm(array):
    return pltpu.with_memory_space_constraint(array, pltpu.HBM)


def on_device(n, side, grads, error, q_start, bucket):
    depth, width = grads.shape[1:]
    rank = q_start.shape[1]
    rows = depth // n
    shares = bucket.shape[1] // n // 128
    vmem = pl.BlockSpec(memory_space=pltpu.VMEM)
    anywhere = pl.BlockSpec(memory_space=pltpu.HBM)
    sds = jax.ShapeDtypeStruct
    dma = pltpu.SemaphoreType.DMA
    comp, p_hat, factor_q, mean = pl.pallas_call(
        functools.partial(iterate_kernel, n, side),
        out_shape=(
            sds((n, rows, width), BF16),
            sds((rank, depth), BF16),
            sds((rank, width), F32),
            sds((shares, 128), F32),
        ),
        in_specs=[anywhere] * 4,
        out_specs=(vmem, vmem, vmem, vmem),
        scratch_shapes=[
            pltpu.VMEM((n, width, rows), BF16),
            pltpu.VMEM((n, rows, width), BF16),
            pltpu.VMEM((n, rows, width), BF16),
            pltpu.VMEM((ITERS, n, rank, rows), BF16),
            pltpu.VMEM((ITERS, n, rank, rows), BF16),
            pltpu.VMEM((ITERS, n, rank, rows), BF16),
            pltpu.VMEM((ITERS, 2, 2, side, rank, width // 2), BF16),
            pltpu.VMEM((rank, width), F32),
            pltpu.VMEM((n, shares, 128), F32),
            pltpu.VMEM((n, shares, 128), BF16),
            pltpu.VMEM((n, shares, 128), BF16),
            dma((2, n)),
            dma((2,)),
            dma((n,)),
            dma((n,)),
            dma((ITERS, n)),
            dma((ITERS, n)),
            dma((ITERS, n)),
            dma((ITERS, n)),
            dma((ITERS, 2, 2, side)),
            dma((ITERS, 2, 2, side)),
        ],
        compiler_params=pltpu.CompilerParams(
            collective_id=0, has_side_effects=True, vmem_limit_bytes=40 << 20
        ),
        name="iterate",
    )(*(in_hbm(a) for a in (grads[0], error[0], q_start.T, bucket.reshape(n, shares, 128))))

    update, new_error, mean = pl.pallas_call(
        output_kernel,
        out_shape=(sds((depth, width), F32), sds((depth, width), BF16), sds((shares, 128), F32)),
        in_specs=[vmem, vmem, vmem, vmem],
        out_specs=(anywhere, anywhere, anywhere),
        scratch_shapes=[
            pltpu.VMEM((4, rows, width), F32),
            pltpu.VMEM((4, rows, width), BF16),
            dma((2, 4)),
            dma,
        ],
        compiler_params=pltpu.CompilerParams(vmem_limit_bytes=16 << 20),
        name="outputs",
    )(comp, p_hat, factor_q, mean)
    return update, new_error[None], mean.reshape(-1)


def solution(mesh):
    n = mesh.shape["dp"]
    side = next(s for s in range(1, n + 1) if s * s == n)
    return jax.shard_map(
        functools.partial(on_device, n, side),
        mesh=mesh,
        in_specs=(
            P("dp", None, "expert"),
            P("dp", None, "expert"),
            P("expert", None),
            P("dp", "expert"),
        ),
        out_specs=(P(None, "expert"), P("dp", None, "expert"), P(("expert", "dp"))),
        check_vma=False,
    )
```

time: 78.6 us -> 60.3 us (0.77)
  Pallas kernels: 72.5 us -> 59.5 us
  local copies, waits for them, and re-layouts: 5.23 us -> 0 us
    pallas_call x1, Pallas kernels: 61.6 us -> 52.7 us  [on_device(): pl.pallas_call(functools.partial(iterate_kernel, n, side), out_shape=(sds...]
    unnamed x7 -> x0, local copies, waits for them, and re-layouts: 5.23 us -> none
    pallas_call x1, Pallas kernels: 10.9 us -> 6.82 us  [on_device(): pl.pallas_call(output_kernel, out_shape=(sds((depth, width), F32), sds((d...]
where the time goes in v2:
time: 60.3 us; the launch traced here: 60.1 us
  Pallas kernels  59.5 us (99%)
  between operations  0.64 us (1%)
    pallas_call x1, Pallas kernels, on_device(): pl.pallas_call(functools.partial(iterate_kernel, n, side), out_shape=(sds...  52.7 us
    pallas_call x1, Pallas kernels, on_device(): pl.pallas_call(output_kernel, out_shape=(sds((depth, width), F32), sds((d...  6.82 us

profile of v2, /device:TPU:0, one launch (start us, length us, event | category | flops | bytes accessed | tf_op | source)
XLA Modules:
  0.0 60.1 jit_solution(12777770927917481839)
XLA Ops:
  0.6 52.7 %iterate.1 = (bf16[16,256,768]{2,1,0:T(8,128)(2,1)S(1)}, bf16[32,4096]{1,0:T(8,128)(2,1)S(1)}, f32[32,768]{1,0:T(8,128)S(1)}, f32[32,128]{1,0:T(8,128)S(1)}) custom-call(bf16[4096,768]{1,0:T(8,128)(2,1)} %bitcast.6, bf16[4096,768]{1,0:T(8,128)(2,1)} %bitcast.7, f32[32,768]{1,0:T(8,128)} %bitcast.9, f32[16,32,128]{2,1,0:T(8,128)} %bitcast.8), custom_call_target="tpu_custom_call" | custom-call | tf_op jit(solution)/shard_map/iterate/pallas_call | solution.py:340
  53.3 6.8 %outputs.1 = (f32[4096,768]{1,0:T(8,128)}, bf16[4096,768]{1,0:T(8,128)(2,1)}, f32[32,128]{1,0:T(8,128)}) custom-call(bf16[16,256,768]{2,1,0:T(8,128)(2,1)S(1)} %get-tuple-element.10.comp, bf16[32,4096]{1,0:T(8,128)(2,1)S(1)} %get-tuple-element.11.p_hat, f32[32,768]{1,0:T(8,128)S(1)} %get-tuple-element.12.factor_q, f32[32,128]{1,0:T(8,128)S(1)} %get-tuple-element.13.mean), custom_call_target="tpu_custom_call" | custom-call | tf_op jit(solution)/shard_map/outputs/pallas_call | solution.py:379

commit v3 on v2

v3 whole, which is shorter than its diff:
```python
import contextlib
import functools

import jax
import jax.numpy as jnp
from jax import lax
from jax.experimental import pallas as pl
from jax.experimental.pallas import tpu as pltpu
from jax.sharding import PartitionSpec as P

ITERS = 2
MESH = pl.DeviceIdType.MESH
F32 = jnp.float32
BF16 = jnp.bfloat16
AHEAD = 6
FIRST_RUNS = (1, 2, 3, 3, 3, 3, 1)
LATER_RUNS = (5, 6, 5)
BARRIER_RUN = 3
TRACE = False


def scope(name):
    return jax.named_scope(name) if TRACE else contextlib.nullcontext()


def runs(items, sizes):
    out = []
    for size in sizes:
        out.append(items[:size])
        items = items[size:]
    assert not items
    return out


def offsets(side):
    near = lambda d: min(d, side - d)
    every = [(dz, dx) for dz in range(side) for dx in range(side) if (dz, dx) != (0, 0)]
    return sorted(every, key=lambda o: (-(near(o[0]) + near(o[1])), o))


def split3(x):
    hi = x.astype(BF16)
    rest = x - hi.astype(F32)
    mid = rest.astype(BF16)
    low = (rest - mid.astype(F32)).astype(BF16)
    return hi, mid, low


def inverse_cholesky(gram, block=8):
    n, lanes, tile = gram.shape[0], 128, 8
    row_id = lax.broadcasted_iota(jnp.int32, (n, lanes), 0)
    lane_id = lax.broadcasted_iota(jnp.int32, (n, lanes), 1)
    eye = (lane_id == row_id + n).astype(F32)
    work = jnp.concatenate([gram, jnp.zeros((n, lanes - n), F32)], axis=1) + eye
    work = [work[tile * i : tile * (i + 1)] for i in range(n // tile)]
    out = [jnp.zeros((tile, lanes), F32) for _ in work]
    tile_row = row_id[:tile]
    for s in range(0, n, block):
        rows = [work[k // tile][k % tile : k % tile + 1] for k in range(s, s + block)]
        pivots = [
            [jnp.broadcast_to(rows[i][:, s + j : s + j + 1], (1, lanes)) for j in range(i + 1)] for i in range(block)
        ]
        rest = range((s + block) // tile, n // tile)
        columns = {
            (t, i): jnp.broadcast_to(work[t][:, s + i : s + i + 1], (tile, lanes)) for t in rest for i in range(block)
        }
        factor, inverse = {}, []
        for p in range(block):
            inverse.append(1.0 / pivots[p][p])
            for i in range(p + 1, block):
                factor[i, p] = pivots[i][p] * inverse[p]
                for j in range(p + 1, i + 1):
                    pivots[i][j] = pivots[i][j] - factor[i, p] * pivots[j][p]
                rows[i] = rows[i] - factor[i, p] * rows[p]
        for p in range(block):
            t, at = divmod(s + p, tile)
            out[t] = jnp.where(tile_row == at, rows[p] / jnp.sqrt(pivots[p][p]), out[t])
        solved = [rows[p] * inverse[p] for p in range(block)]
        for p in reversed(range(block)):
            for i in range(p + 1, block):
                solved[p] = solved[p] - factor[i, p] * solved[i]
        for t in rest:
            for i in range(block):
                work[t] = work[t] - columns[t, i] * solved[i]
    return jnp.concatenate(out, axis=0)[:, n : 2 * n]


def group_of(side):
    me = lax.axis_index("dp")
    my_z, my_x = lax.div(me, side), lax.rem(me, side)
    peers = [lax.rem(my_z + dz, side) * side + lax.rem(my_x + dx, side) for dz, dx in offsets(side)]
    return me, my_z, my_x, peers


def iterate_kernel(
    n,
    side,
    grads,
    error,
    q_start,
    bucket,
    comp,
    p_out,
    q_out,
    mean_out,
    comp_t,
    ge_buf,
    p_send,
    p_recv,
    p_all,
    q_x,
    q0_buf,
    b0_buf,
    b_buf,
    b_recv,
    load_sem,
    small_sem,
    send_sem,
    b_recv_sem,
    rs_recv_sem,
    ag_recv_sem,
    q_recv_sem,
):
    me, my_z, my_x, peers = group_of(side)
    every = peers + [me]
    own = n - 1
    order = offsets(side)
    back = [order.index(((side - dz) % side, (side - dx) % side)) for dz, dx in order]
    steps = [min(dz, side - dz) + min(dx, side - dx) for dz, dx in order]
    rings = [[i for i in range(own) if steps[i] == step] for step in sorted(set(steps), reverse=True)]
    ring_of = [next(r for r, ring in enumerate(rings) if i in ring) for i in range(own)]
    rows = comp.shape[1]
    rank = q_start.shape[0]
    inv_n = 1.0 / n

    def remote(src, dst, send, recv, peer):
        return pltpu.make_async_remote_copy(
            src_ref=src, dst_ref=dst, send_sem=send, recv_sem=recv, device_id={"dp": peer}, device_id_type=MESH
        )

    barrier = pltpu.get_barrier_semaphore()
    for peer in peers:
        pl.semaphore_signal(barrier, inc=1, device_id={"dp": peer}, device_id_type=MESH)

    first_runs = runs(list(range(n)), FIRST_RUNS)
    run_of = [next(r for r, run in enumerate(first_runs) if i in run) for i in range(n)]

    def load(i):
        part = pl.ds(pl.multiple_of(every[i] * rows, rows), rows)
        for k, source in enumerate((grads, error)):
            pltpu.make_async_copy(source.at[part], ge_buf.at[i, k], load_sem.at[run_of[i]]).start()

    def loaded(r):
        held = ge_buf.at[pl.ds(first_runs[r][0], len(first_runs[r]))]
        pltpu.make_async_copy(held, held, load_sem.at[r]).wait()

    small = (
        pltpu.make_async_copy(q_start, q0_buf, small_sem.at[0]),
        pltpu.make_async_copy(bucket, b0_buf, small_sem.at[1]),
    )
    for i in range(AHEAD):
        load(i)
        if i == 0:
            small[0].start()

    def rs_send(it, i):
        remote(
            p_send.at[it, i], p_recv.at[it, back[i]], send_sem.at[0], rs_recv_sem.at[it, ring_of[i]], peers[i]
        ).start()

    def rs_wait(it, r):
        held = p_recv.at[it, pl.ds(rings[r][0], len(rings[r]))]
        remote(held, held, send_sem.at[0], rs_recv_sem.at[it, r], peers[0]).wait_recv()

    def ag_send(it, i):
        held = p_all.at[it, me]
        remote(held, held, send_sem.at[1], ag_recv_sem.at[it, ring_of[i]], peers[i]).start()

    def ag_wait(it, r):
        held = p_all.at[it, pl.ds(0, len(rings[r]))]
        remote(held, held, send_sem.at[1], ag_recv_sem.at[it, r], peers[0]).wait_recv()

    for it in range(ITERS):
        def multiply(run):
            blocks = [jnp.dot(q_half, comp_t[i], preferred_element_type=F32) for i in run]
            for i, part in zip(run, blocks):
                if i != own:
                    p_send[it, i] = part.astype(BF16)
            return blocks[-1]

        def send(run):
            for i in run:
                if i != own:
                    rs_send(it, i)

        with scope(f"p_local{it}"):
            if it == 0:
                before, ready = [], []
                for r, run in enumerate(first_runs):
                    with scope("load"):
                        loaded(r)
                        for i in range(AHEAD + run[0], min(AHEAD + run[-1] + 1, n)):
                            load(i)
                        if r == 1:
                            small[0].wait()
                            q_half = q0_buf[...].astype(BF16)
                    for i in run:
                        comp[i] = ge_buf[i, 0] + ge_buf[i, 1]
                        comp_t[i] = comp[i].T
                    if before:
                        multiply(before)
                        ready = ready + before
                    before = run
                    if r == BARRIER_RUN:
                        small[1].start()
                        with scope("entry"):
                            pl.semaphore_wait(barrier, n - 1)
                    if r >= BARRIER_RUN:
                        send(ready)
                        ready = []
                total = multiply(before)
                send(before)
            else:
                for run in runs(list(range(n)), LATER_RUNS):
                    total = multiply(run)
                    send(run)
        if it == ITERS - 1:
            with scope("bucket"):
                remote(b_recv, b_recv, send_sem.at[2], b_recv_sem, peers[0]).wait_recv()
                share = b_buf[me].astype(F32)
                for i in range(own):
                    share = share + b_recv[i].astype(F32)
                mean_out[...] = share * inv_n
        with scope(f"rs{it}"):
            for r in reversed(range(len(rings))):
                rs_wait(it, r)
                for i in rings[r]:
                    total = total + p_recv[it, i].astype(F32)
            p_all[it, me] = (total * inv_n).astype(BF16)

        with scope(f"ag{it}"):
            for i in range(own):
                ag_send(it, i)
            raw_q = jnp.dot(p_all[it, me], comp[own], preferred_element_type=F32)
            for r in reversed(range(len(rings))):
                ag_wait(it, r)
                for i in rings[r]:
                    raw_q = raw_q + jnp.dot(p_all[it, peers[i]], comp[i], preferred_element_type=F32)
            gram = jnp.zeros((rank, rank), F32)
            for j in range(n):
                part = p_all[it, j]
                gram = gram + lax.dot_general(part, part, (((1,), (1,)), ((), ())), preferred_element_type=F32)
        if it == 0:
            with scope("bucket"):
                small[1].wait()
                b_buf[...] = b0_buf[...].astype(BF16)
                for i, peer in enumerate(peers):
                    remote(b_buf.at[peer], b_recv.at[back[i]], send_sem.at[2], b_recv_sem, peer).start()
        with scope(f"cholesky{it}"):
            inverse = inverse_cholesky(gram)

        half = comp.shape[2] // 2

        def q_start_half(stage, h, part):
            along_x = (h + stage) % 2 == 0
            mine_at = my_x if along_x else my_z
            slot = q_x.at[it, stage, h, mine_at]
            slot[...] = part.astype(BF16)
            for d in (2, 1, 3):
                at = lax.rem(mine_at + d, side)
                peer = my_z * side + at if along_x else at * side + my_x
                remote(slot, slot, send_sem.at[3], q_recv_sem.at[it, stage, h], peer).start()

        def q_sum_half(stage, h):
            with scope(f"q_wait{it}_{stage}"):
                held = q_x.at[it, stage, h, pl.ds(0, side - 1)]
                remote(held, held, send_sem.at[3], q_recv_sem.at[it, stage, h], peers[0]).wait_recv()
            return sum(q_x[it, stage, h, s].astype(F32) for s in range(side))

        with scope(f"q_send{it}"):
            for h in range(2):
                part = jnp.dot(
                    inverse,
                    raw_q[:, h * half : (h + 1) * half],
                    preferred_element_type=F32,
                    precision=lax.Precision.HIGHEST,
                )
                q_start_half(0, h, part)
        if it == ITERS - 1:
            with scope("p_hat"):
                pieces = split3(inverse)
                for i in range(n):
                    block = p_all[it, every[i]]
                    p_hat = sum(jnp.dot(piece, block, preferred_element_type=F32) for piece in pieces)
                    p_hat = p_hat.T.astype(BF16)
                    p_out[i] = jnp.concatenate([p_hat, p_hat, p_hat], axis=1)
        for h in range(2):
            q_start_half(1, h, q_sum_half(0, h))
        parts = [q_sum_half(1, h) for h in range(2)]
        factor_q = jnp.concatenate(parts, axis=1) * inv_n
        if it + 1 < ITERS:
            factor_q = factor_q / jnp.sqrt(jnp.sum(factor_q * factor_q, axis=1, keepdims=True) + 1e-06)
            q_half = factor_q.astype(BF16)
        else:
            q_out[...] = factor_q

    with scope("sends"):
        blocks = p_all.at[:, pl.ds(0, own)]
        shares = b_buf.at[pl.ds(0, own)]
        halves = q_x.at[:, :, :, pl.ds(0, side - 1)]
        for k, (held, arrived) in enumerate(
            (
                (p_send, rs_recv_sem.at[0, 0]),
                (blocks, ag_recv_sem.at[0, 0]),
                (shares, b_recv_sem),
                (halves, q_recv_sem.at[0, 0, 0]),
            )
        ):
            remote(held, held, send_sem.at[k], arrived, peers[0]).wait_send()


def output_kernel(
    side, comp, p_hat, factor_q, mean, update, new_error, mean_out, u_buf, n_buf, sem, mean_sem
):
    me, _, _, peers = group_of(side)
    every = peers + [me]
    n, rows, _ = comp.shape
    mean_copy = pltpu.make_async_copy(mean, mean_out, mean_sem)
    mean_copy.start()
    right = jnp.concatenate(split3(factor_q[...]), axis=0)
    slots = u_buf.shape[0]
    small = rows // 2
    steps = [[(0, 0, small)], [(0, small, small)], [(1, 0, rows)]]
    steps += [[(i, 0, rows), (i + 1, 0, rows)] for i in range(2, n, 2)]

    def stored(k):
        slot, size = k % slots, pl.ds(0, sum(piece[2] for piece in steps[k]))
        for which, held in enumerate((u_buf.at[slot, size], n_buf.at[slot, size])):
            pltpu.make_async_copy(held, held, sem.at[which, slot]).wait()

    for k, step in enumerate(steps):
        slot = k % slots
        if k >= slots:
            with scope("stores"):
                stored(k - slots)
        with scope("block"):
            at = 0
            for i, r, size in step:
                value = jnp.dot(p_hat[i, r : r + size], right, preferred_element_type=F32)
                u_buf[slot, at : at + size] = value
                n_buf[slot, at : at + size] = (comp[i, r : r + size].astype(F32) - value).astype(BF16)
                at += size
        at = 0
        for i, r, size in step:
            part = pl.ds(pl.multiple_of(every[i] * rows + r, size), size)
            held = pl.ds(at, size)
            pltpu.make_async_copy(u_buf.at[slot, held], update.at[part], sem.at[0, slot]).start()
            pltpu.make_async_copy(n_buf.at[slot, held], new_error.at[part], sem.at[1, slot]).start()
            at += size
    with scope("last"):
        for k in range(max(0, len(steps) - slots), len(steps)):
            stored(k)
    mean_copy.wait()


def in_hbm(array):
    return pltpu.with_memory_space_constraint(array, pltpu.HBM)


def on_device(n, side, grads, error, q_start, bucket):
    depth, width = grads.shape[1:]
    rank = q_start.shape[1]
    rows = depth // n
    shares = bucket.shape[1] // n // 128
    vmem = pl.BlockSpec(memory_space=pltpu.VMEM)
    anywhere = pl.BlockSpec(memory_space=pltpu.HBM)
    sds = jax.ShapeDtypeStruct
    dma = pltpu.SemaphoreType.DMA
    comp, p_hat, factor_q, mean = pl.pallas_call(
        functools.partial(iterate_kernel, n, side),
        out_shape=(
            sds((n, rows, width), BF16),
            sds((n, rows, 3 * rank), BF16),
            sds((rank, width), F32),
            sds((shares, 128), F32),
        ),
        in_specs=[anywhere] * 4,
        out_specs=(vmem, vmem, vmem, vmem),
        scratch_shapes=[
            pltpu.VMEM((n, width, rows), BF16),
            pltpu.VMEM((n, 2, rows, width), BF16),
            pltpu.VMEM((ITERS, n - 1, rank, rows), BF16),
            pltpu.VMEM((ITERS, n - 1, rank, rows), BF16),
            pltpu.VMEM((ITERS, n, rank, rows), BF16),
            pltpu.VMEM((ITERS, 2, 2, side, rank, width // 2), BF16),
            pltpu.VMEM((rank, width), F32),
            pltpu.VMEM((n, shares, 128), F32),
            pltpu.VMEM((n, shares, 128), BF16),
            pltpu.VMEM((n - 1, shares, 128), BF16),
            dma((len(FIRST_RUNS),)),
            dma((2,)),
            dma((4,)),
            dma,
            dma((ITERS, 4)),
            dma((ITERS, 4)),
            dma((ITERS, 2, 2)),
        ],
        compiler_params=pltpu.CompilerParams(
            collective_id=0, has_side_effects=True, vmem_limit_bytes=40 << 20
        ),
        name="iterate",
    )(*(in_hbm(a) for a in (grads[0], error[0], q_start.T, bucket.reshape(n, shares, 128))))

    update, new_error, mean = pl.pallas_call(
        functools.partial(output_kernel, side),
        out_shape=(sds((depth, width), F32), sds((depth, width), BF16), sds((shares, 128), F32)),
        in_specs=[vmem, vmem, vmem, vmem],
        out_specs=(anywhere, anywhere, anywhere),
        scratch_shapes=[
            pltpu.VMEM((4, 2 * rows, width), F32),
            pltpu.VMEM((4, 2 * rows, width), BF16),
            dma((2, 4)),
            dma,
        ],
        compiler_params=pltpu.CompilerParams(vmem_limit_bytes=16 << 20),
        name="outputs",
    )(comp, p_hat, factor_q, mean)
    return update, new_error[None], mean.reshape(-1)


def solution(mesh):
    n = mesh.shape["dp"]
    side = next(s for s in range(1, n + 1) if s * s == n)
    return jax.shard_map(
        functools.partial(on_device, n, side),
        mesh=mesh,
        in_specs=(
            P("dp", None, "expert"),
            P("dp", None, "expert"),
            P("expert", None),
            P("dp", "expert"),
        ),
        out_specs=(P(None, "expert"), P("dp", None, "expert"), P(("expert", "dp"))),
        check_vma=False,
    )
```

time: 60.3 us -> 57.8 us (0.959)
  Pallas kernels: 59.5 us -> 57 us
    pallas_call x1, Pallas kernels: 52.7 us -> 50.3 us  [on_device(): pl.pallas_call(functools.partial(iterate_kernel, n, side), out_shape=(sds...]
where the time goes in v3:
time: 57.8 us; the launch traced here: 57.7 us
  Pallas kernels  57 us (99%)
  between operations  0.64 us (1%)
    pallas_call x1, Pallas kernels, on_device(): pl.pallas_call(functools.partial(iterate_kernel, n, side), out_shape=(sds...  50.3 us
    pallas_call x1, Pallas kernels, on_device(): pl.pallas_call(functools.partial(output_kernel, side), out_shape=(sds((de...  6.71 us

profile of v3, /device:TPU:0, one launch (start us, length us, event | category | flops | bytes accessed | tf_op | source)
XLA Modules:
  0.0 57.7 jit_solution(7552376709096370403)
XLA Ops:
  0.6 50.3 %iterate.1 = (bf16[16,256,768]{2,1,0:T(8,128)(2,1)S(1)}, bf16[16,256,96]{2,1,0:T(8,128)(2,1)S(1)}, f32[32,768]{1,0:T(8,128)S(1)}, f32[32,128]{1,0:T(8,128)S(1)}) custom-call(bf16[4096,768]{1,0:T(8,128)(2,1)} %bitcast.6, bf16[4096,768]{1,0:T(8,128)(2,1)} %bitcast.7, f32[32,768]{1,0:T(8,128)} %bitcast.9, f32[16,32,128]{2,1,0:T(8,128)} %bitcast.8), custom_call_target="tpu_custom_call" | custom-call | tf_op jit(solution)/shard_map/iterate/pallas_call | solution.py:379
  51.0 6.7 %outputs.1 = (f32[4096,768]{1,0:T(8,128)}, bf16[4096,768]{1,0:T(8,128)(2,1)}, f32[32,128]{1,0:T(8,128)}) custom-call(bf16[16,256,768]{2,1,0:T(8,128)(2,1)S(1)} %get-tuple-element.10.comp, bf16[16,256,96]{2,1,0:T(8,128)(2,1)S(1)} %get-tuple-element.11.p_hat, f32[32,768]{1,0:T(8,128)S(1)} %get-tuple-element.12.factor_q, f32[32,128]{1,0:T(8,128)S(1)} %get-tuple-element.13.mean), custom_call_target="tpu_custom_call" | custom-call | tf_op jit(solution)/shard_map/outputs/pallas_call | solution.py:414

commit v4 on v3

--- a/solution.py
+++ b/solution.py
@@ -13,7 +13,7 @@
 F32 = jnp.float32
 BF16 = jnp.bfloat16
 AHEAD = 6
-FIRST_RUNS = (1, 2, 3, 3, 3, 3, 1)
+FIRST_RUNS = (2, 2, 2, 2, 2, 2, 2, 2)
 LATER_RUNS = (5, 6, 5)
 BARRIER_RUN = 3
 TRACE = False
@@ -50,7 +50,7 @@
     n, lanes, tile = gram.shape[0], 128, 8
     row_id = lax.broadcasted_iota(jnp.int32, (n, lanes), 0)
     lane_id = lax.broadcasted_iota(jnp.int32, (n, lanes), 1)
-    eye = (lane_id == row_id + n).astype(F32)
+    eye = ((lane_id >= n) & (lane_id % n == row_id)).astype(F32)
     work = jnp.concatenate([gram, jnp.zeros((n, lanes - n), F32)], axis=1) + eye
     work = [work[tile * i : tile * (i + 1)] for i in range(n // tile)]
     out = [jnp.zeros((tile, lanes), F32) for _ in work]
@@ -82,7 +82,15 @@
         for t in rest:
             for i in range(block):
                 work[t] = work[t] - columns[t, i] * solved[i]
-    return jnp.concatenate(out, axis=0)[:, n : 2 * n]
+    return jnp.concatenate(out, axis=0)
+
+
+def terms_in_lanes(inverse):
+    n = inverse.shape[0]
+    part = lax.broadcasted_iota(jnp.int32, inverse.shape, 1) // n
+    hi, mid, low = (x.astype(F32) for x in split3(jnp.where(part == 0, 0.0, inverse)))
+    start = jnp.where(part == 1, hi, jnp.where(part == 2, mid, 0.0))
+    return jnp.where(part == 3, low, start).astype(BF16), jnp.where(part == 3, hi, start).astype(BF16)
 
 
 def group_of(side):
@@ -212,25 +220,19 @@
                         ready = ready + before
                     before = run
                     if r == BARRIER_RUN:
-                        small[1].start()
                         with scope("entry"):
                             pl.semaphore_wait(barrier, n - 1)
                     if r >= BARRIER_RUN:
                         send(ready)
                         ready = []
+                    if r == len(first_runs) - 2:
+                        small[1].start()
                 total = multiply(before)
                 send(before)
             else:
                 for run in runs(list(range(n)), LATER_RUNS):
                     total = multiply(run)
                     send(run)
-        if it == ITERS - 1:
-            with scope("bucket"):
-                remote(b_recv, b_recv, send_sem.at[2], b_recv_sem, peers[0]).wait_recv()
-                share = b_buf[me].astype(F32)
-                for i in range(own):
-                    share = share + b_recv[i].astype(F32)
-                mean_out[...] = share * inv_n
         with scope(f"rs{it}"):
             for r in reversed(range(len(rings))):
                 rs_wait(it, r)
@@ -239,25 +241,25 @@
             p_all[it, me] = (total * inv_n).astype(BF16)
 
         with scope(f"ag{it}"):
-            for i in range(own):
-                ag_send(it, i)
+            near, others = len(rings) - 1, list(range(len(rings) - 1))
+            for r in others[:1] + [near] + others[1:]:
+                for i in rings[r]:
+                    ag_send(it, i)
             raw_q = jnp.dot(p_all[it, me], comp[own], preferred_element_type=F32)
-            for r in reversed(range(len(rings))):
+            ag_wait(it, near)
+            for i in rings[near]:
+                raw_q = raw_q + jnp.dot(p_all[it, peers[i]], comp[i], preferred_element_type=F32)
+            for r in others:
                 ag_wait(it, r)
-                for i in rings[r]:
-                    raw_q = raw_q + jnp.dot(p_all[it, peers[i]], comp[i], preferred_element_type=F32)
+        with scope(f"cholesky{it}"):
             gram = jnp.zeros((rank, rank), F32)
             for j in range(n):
                 part = p_all[it, j]
                 gram = gram + lax.dot_general(part, part, (((1,), (1,)), ((), ())), preferred_element_type=F32)
-        if it == 0:
-            with scope("bucket"):
-                small[1].wait()
-                b_buf[...] = b0_buf[...].astype(BF16)
-                for i, peer in enumerate(peers):
-                    remote(b_buf.at[peer], b_recv.at[back[i]], send_sem.at[2], b_recv_sem, peer).start()
-        with scope(f"cholesky{it}"):
-            inverse = inverse_cholesky(gram)
+            terms = terms_in_lanes(inverse_cholesky(gram))
+            for r in others:
+                for i in rings[r]:
+                    raw_q = raw_q + jnp.dot(p_all[it, peers[i]], comp[i], preferred_element_type=F32)
 
         half = comp.shape[2] // 2
 
@@ -278,22 +280,24 @@
             return sum(q_x[it, stage, h, s].astype(F32) for s in range(side))
 
         with scope(f"q_send{it}"):
+            left = jnp.concatenate(terms, axis=1)
+            hi, mid, low = split3(raw_q)
+            zero = jnp.zeros_like(hi)
+            right = jnp.concatenate([zero, hi, hi, hi, zero, mid, mid, low], axis=0)
             for h in range(2):
-                part = jnp.dot(
-                    inverse,
-                    raw_q[:, h * half : (h + 1) * half],
-                    preferred_element_type=F32,
-                    precision=lax.Precision.HIGHEST,
-                )
+                part = jnp.dot(left, right[:, h * half : (h + 1) * half], preferred_element_type=F32)
                 q_start_half(0, h, part)
         if it == ITERS - 1:
             with scope("p_hat"):
-                pieces = split3(inverse)
                 for i in range(n):
                     block = p_all[it, every[i]]
-                    p_hat = sum(jnp.dot(piece, block, preferred_element_type=F32) for piece in pieces)
-                    p_hat = p_hat.T.astype(BF16)
+                    block = jnp.concatenate([jnp.zeros_like(block), block, block, block], axis=0)
+                    p_hat = jnp.dot(terms[0], block, preferred_element_type=F32).T.astype(BF16)
                     p_out[i] = jnp.concatenate([p_hat, p_hat, p_hat], axis=1)
+            small[1].wait()
+            b_buf[...] = b0_buf[...].astype(BF16)
+            for i, peer in enumerate(peers):
+                remote(b_buf.at[peer], b_recv.at[back[i]], send_sem.at[2], b_recv_sem, peer).start()
         for h in range(2):
             q_start_half(1, h, q_sum_half(0, h))
         parts = [q_sum_half(1, h) for h in range(2)]
@@ -304,6 +308,12 @@
         else:
             q_out[...] = factor_q
 
+    with scope("bucket"):
+        remote(b_recv, b_recv, send_sem.at[2], b_recv_sem, peers[0]).wait_recv()
+        share = b_buf[me].astype(F32)
+        for i in range(own):
+            share = share + b_recv[i].astype(F32)
+        mean_out[...] = share * inv_n
     with scope("sends"):
         blocks = p_all.at[:, pl.ds(0, own)]
         shares = b_buf.at[pl.ds(0, own)]

time: 57.8 us -> 56.2 us (0.972)
  Pallas kernels: 57 us -> 55.4 us
    pallas_call x1, Pallas kernels: 50.3 us -> 48.7 us  [on_device(): pl.pallas_call(functools.partial(iterate_kernel, n, side), out_shape=(sds...]
where the time goes in v4:
time: 56.2 us; the launch traced here: 56 us
  Pallas kernels  55.4 us (99%)
  between operations  0.64 us (1%)
    pallas_call x1, Pallas kernels, on_device(): pl.pallas_call(functools.partial(iterate_kernel, n, side), out_shape=(sds...  48.7 us
    pallas_call x1, Pallas kernels, on_device(): pl.pallas_call(functools.partial(output_kernel, side), out_shape=(sds((de...  6.71 us

profile of v4, /device:TPU:0, one launch (start us, length us, event | category | flops | bytes accessed | tf_op | source)
XLA Modules:
  0.0 56.0 jit_solution(17113004331709955441)
XLA Ops:
  0.6 48.7 %iterate.1 = (bf16[16,256,768]{2,1,0:T(8,128)(2,1)S(1)}, bf16[16,256,96]{2,1,0:T(8,128)(2,1)S(1)}, f32[32,768]{1,0:T(8,128)S(1)}, f32[32,128]{1,0:T(8,128)S(1)}) custom-call(bf16[4096,768]{1,0:T(8,128)(2,1)} %bitcast.6, bf16[4096,768]{1,0:T(8,128)(2,1)} %bitcast.7, f32[32,768]{1,0:T(8,128)} %bitcast.9, f32[16,32,128]{2,1,0:T(8,128)} %bitcast.8), custom_call_target="tpu_custom_call" | custom-call | tf_op jit(solution)/shard_map/iterate/pallas_call | solution.py:389
  49.3 6.7 %outputs.1 = (f32[4096,768]{1,0:T(8,128)}, bf16[4096,768]{1,0:T(8,128)(2,1)}, f32[32,128]{1,0:T(8,128)}) custom-call(bf16[16,256,768]{2,1,0:T(8,128)(2,1)S(1)} %get-tuple-element.10.comp, bf16[16,256,96]{2,1,0:T(8,128)(2,1)S(1)} %get-tuple-element.11.p_hat, f32[32,768]{1,0:T(8,128)S(1)} %get-tuple-element.12.factor_q, f32[32,128]{1,0:T(8,128)S(1)} %get-tuple-element.13.mean), custom_call_target="tpu_custom_call" | custom-call | tf_op jit(solution)/shard_map/outputs/pallas_call | solution.py:424

commit v5 on v4

--- a/solution.py
+++ b/solution.py
@@ -14,8 +14,8 @@
 BF16 = jnp.bfloat16
 AHEAD = 6
 FIRST_RUNS = (2, 2, 2, 2, 2, 2, 2, 2)
-LATER_RUNS = (5, 6, 5)
-BARRIER_RUN = 3
+LATER_RUNS = (3, 4, 4, 5)
+BARRIER_RUN = 1
 TRACE = False
 
 
@@ -151,16 +151,17 @@
         pl.semaphore_signal(barrier, inc=1, device_id={"dp": peer}, device_id_type=MESH)
 
     first_runs = runs(list(range(n)), FIRST_RUNS)
+    in_flight = load_sem.shape[0]
     run_of = [next(r for r, run in enumerate(first_runs) if i in run) for i in range(n)]
 
     def load(i):
         part = pl.ds(pl.multiple_of(every[i] * rows, rows), rows)
         for k, source in enumerate((grads, error)):
-            pltpu.make_async_copy(source.at[part], ge_buf.at[i, k], load_sem.at[run_of[i]]).start()
+            pltpu.make_async_copy(source.at[part], ge_buf.at[i, k], load_sem.at[run_of[i] % in_flight]).start()
 
     def loaded(r):
         held = ge_buf.at[pl.ds(first_runs[r][0], len(first_runs[r]))]
-        pltpu.make_async_copy(held, held, load_sem.at[r]).wait()
+        pltpu.make_async_copy(held, held, load_sem.at[r % in_flight]).wait()
 
     small = (
         pltpu.make_async_copy(q_start, q0_buf, small_sem.at[0]),
@@ -173,20 +174,17 @@
 
     def rs_send(it, i):
         remote(
-            p_send.at[it, i], p_recv.at[it, back[i]], send_sem.at[0], rs_recv_sem.at[it, ring_of[i]], peers[i]
+            p_send.at[it, i], p_recv.at[it, back[i]], send_sem.at[0], rs_recv_sem.at[it], peers[i]
         ).start()
-
-    def rs_wait(it, r):
-        held = p_recv.at[it, pl.ds(rings[r][0], len(rings[r]))]
-        remote(held, held, send_sem.at[0], rs_recv_sem.at[it, r], peers[0]).wait_recv()
 
     def ag_send(it, i):
         held = p_all.at[it, me]
-        remote(held, held, send_sem.at[1], ag_recv_sem.at[it, ring_of[i]], peers[i]).start()
-
-    def ag_wait(it, r):
-        held = p_all.at[it, pl.ds(0, len(rings[r]))]
-        remote(held, held, send_sem.at[1], ag_recv_sem.at[it, r], peers[0]).wait_recv()
+        remote(held, held, send_sem.at[1], ag_recv_sem.at[it, int(ring_of[i] == len(rings) - 1)], peers[i]).start()
+
+    def ag_wait(it, near):
+        count = len(rings[-1]) if near else own - len(rings[-1])
+        held = p_all.at[it, pl.ds(0, count)]
+        remote(held, held, send_sem.at[1], ag_recv_sem.at[it, near], peers[0]).wait_recv()
 
     for it in range(ITERS):
         def multiply(run):
@@ -234,10 +232,9 @@
                     total = multiply(run)
                     send(run)
         with scope(f"rs{it}"):
-            for r in reversed(range(len(rings))):
-                rs_wait(it, r)
-                for i in rings[r]:
-                    total = total + p_recv[it, i].astype(F32)
+            remote(p_recv.at[it], p_recv.at[it], send_sem.at[0], rs_recv_sem.at[it], peers[0]).wait_recv()
+            for i in range(own):
+                total = total + p_recv[it, i].astype(F32)
             p_all[it, me] = (total * inv_n).astype(BF16)
 
         with scope(f"ag{it}"):
@@ -246,11 +243,10 @@
                 for i in rings[r]:
                     ag_send(it, i)
             raw_q = jnp.dot(p_all[it, me], comp[own], preferred_element_type=F32)
-            ag_wait(it, near)
+            ag_wait(it, 1)
             for i in rings[near]:
                 raw_q = raw_q + jnp.dot(p_all[it, peers[i]], comp[i], preferred_element_type=F32)
-            for r in others:
-                ag_wait(it, r)
+            ag_wait(it, 0)
         with scope(f"cholesky{it}"):
             gram = jnp.zeros((rank, rank), F32)
             for j in range(n):
@@ -303,7 +299,7 @@
         parts = [q_sum_half(1, h) for h in range(2)]
         factor_q = jnp.concatenate(parts, axis=1) * inv_n
         if it + 1 < ITERS:
-            factor_q = factor_q / jnp.sqrt(jnp.sum(factor_q * factor_q, axis=1, keepdims=True) + 1e-06)
+            factor_q = factor_q * (1.0 / jnp.sqrt(jnp.sum(factor_q * factor_q, axis=1, keepdims=True) + 1e-06))
             q_half = factor_q.astype(BF16)
         else:
             q_out[...] = factor_q
@@ -320,7 +316,7 @@
         halves = q_x.at[:, :, :, pl.ds(0, side - 1)]
         for k, (held, arrived) in enumerate(
             (
-                (p_send, rs_recv_sem.at[0, 0]),
+                (p_send, rs_recv_sem.at[0]),
                 (blocks, ag_recv_sem.at[0, 0]),
                 (shares, b_recv_sem),
                 (halves, q_recv_sem.at[0, 0, 0]),
@@ -407,12 +403,12 @@
             pltpu.VMEM((n, shares, 128), F32),
             pltpu.VMEM((n, shares, 128), BF16),
             pltpu.VMEM((n - 1, shares, 128), BF16),
-            dma((len(FIRST_RUNS),)),
+            dma((AHEAD // FIRST_RUNS[0],)),
             dma((2,)),
             dma((4,)),
             dma,
-            dma((ITERS, 4)),
-            dma((ITERS, 4)),
+            dma((ITERS,)),
+            dma((ITERS, 2)),
             dma((ITERS, 2, 2)),
         ],
         compiler_params=pltpu.CompilerParams(

time: 56.2 us -> 55.9 us (level)
  no operation moved by 1% of the time
where the time goes in v5:
time: 55.9 us; the launch traced here: 55.8 us
  Pallas kernels  55.2 us (99%)
  between operations  0.64 us (1%)
    pallas_call x1, Pallas kernels, on_device(): pl.pallas_call(functools.partial(iterate_kernel, n, side), out_shape=(sds...  48.4 us
    pallas_call x1, Pallas kernels, on_device(): pl.pallas_call(functools.partial(output_kernel, side), out_shape=(sds((de...  6.71 us

profile of v5, /device:TPU:0, one launch (start us, length us, event | category | flops | bytes accessed | tf_op | source)
XLA Modules:
  0.0 55.8 jit_solution(17835944374259814556)
XLA Ops:
  0.6 48.4 %iterate.1 = (bf16[16,256,768]{2,1,0:T(8,128)(2,1)S(1)}, bf16[16,256,96]{2,1,0:T(8,128)(2,1)S(1)}, f32[32,768]{1,0:T(8,128)S(1)}, f32[32,128]{1,0:T(8,128)S(1)}) custom-call(bf16[4096,768]{1,0:T(8,128)(2,1)} %bitcast.6, bf16[4096,768]{1,0:T(8,128)(2,1)} %bitcast.7, f32[32,768]{1,0:T(8,128)} %bitcast.9, f32[16,32,128]{2,1,0:T(8,128)} %bitcast.8), custom_call_target="tpu_custom_call" | custom-call | tf_op jit(solution)/shard_map/iterate/pallas_call | solution.py:385
  49.1 6.7 %outputs.1 = (f32[4096,768]{1,0:T(8,128)}, bf16[4096,768]{1,0:T(8,128)(2,1)}, f32[32,128]{1,0:T(8,128)}) custom-call(bf16[16,256,768]{2,1,0:T(8,128)(2,1)S(1)} %get-tuple-element.10.comp, bf16[16,256,96]{2,1,0:T(8,128)(2,1)S(1)} %get-tuple-element.11.p_hat, f32[32,768]{1,0:T(8,128)S(1)} %get-tuple-element.12.factor_q, f32[32,128]{1,0:T(8,128)S(1)} %get-tuple-element.13.mean), custom_call_target="tpu_custom_call" | custom-call | tf_op jit(solution)/shard_map/outputs/pallas_call | solution.py:420

commit v6 on v4

--- a/solution.py
+++ b/solution.py
@@ -14,8 +14,8 @@
 BF16 = jnp.bfloat16
 AHEAD = 6
 FIRST_RUNS = (2, 2, 2, 2, 2, 2, 2, 2)
-LATER_RUNS = (5, 6, 5)
-BARRIER_RUN = 3
+LATER_RUNS = (3, 4, 4, 5)
+BARRIER_RUN = 1
 TRACE = False
 
 

time: 56.2 us -> 55.9 us (level)
  no operation moved by 1% of the time
where the time goes in v6:
time: 55.9 us; the launch traced here: 55.7 us
  Pallas kernels  55.1 us (99%)
  between operations  0.64 us (1%)
    pallas_call x1, Pallas kernels, on_device(): pl.pallas_call(functools.partial(iterate_kernel, n, side), out_shape=(sds...  48.4 us
    pallas_call x1, Pallas kernels, on_device(): pl.pallas_call(functools.partial(output_kernel, side), out_shape=(sds((de...  6.71 us

profile of v6, /device:TPU:0, one launch (start us, length us, event | category | flops | bytes accessed | tf_op | source)
XLA Modules:
  0.0 55.7 jit_solution(16139223252276790509)
XLA Ops:
  0.6 48.4 %iterate.1 = (bf16[16,256,768]{2,1,0:T(8,128)(2,1)S(1)}, bf16[16,256,96]{2,1,0:T(8,128)(2,1)S(1)}, f32[32,768]{1,0:T(8,128)S(1)}, f32[32,128]{1,0:T(8,128)S(1)}) custom-call(bf16[4096,768]{1,0:T(8,128)(2,1)} %bitcast.6, bf16[4096,768]{1,0:T(8,128)(2,1)} %bitcast.7, f32[32,768]{1,0:T(8,128)} %bitcast.9, f32[16,32,128]{2,1,0:T(8,128)} %bitcast.8), custom_call_target="tpu_custom_call" | custom-call | tf_op jit(solution)/shard_map/iterate/pallas_call | solution.py:389
  49.0 6.7 %outputs.1 = (f32[4096,768]{1,0:T(8,128)}, bf16[4096,768]{1,0:T(8,128)(2,1)}, f32[32,128]{1,0:T(8,128)}) custom-call(bf16[16,256,768]{2,1,0:T(8,128)(2,1)S(1)} %get-tuple-element.10.comp, bf16[16,256,96]{2,1,0:T(8,128)(2,1)S(1)} %get-tuple-element.11.p_hat, f32[32,768]{1,0:T(8,128)S(1)} %get-tuple-element.12.factor_q, f32[32,128]{1,0:T(8,128)S(1)} %get-tuple-element.13.mean), custom_call_target="tpu_custom_call" | custom-call | tf_op jit(solution)/shard_map/outputs/pallas_call | solution.py:424
